TPU v7x, 32 devices: a whole 2x2x4 slice. The times are simulated.
32 devices in a mesh: seq: 16 (over z, x, core), head: 2 (over y).
Axes of the slice: x: 2, y: 2, z: 4, core: 2. Of those that a mesh axis runs over, the one named last changes fastest.
Arguments:
- queries: bfloat16 [8192, 8192], P('seq', 'head'), may hold values from -6 to 6
- key_rows: bfloat16 [8192, 8192], P('seq', 'head'), may hold values from -6 to 6
- values: bfloat16 [8192, 8192], P('seq', 'head'), may hold values from -360 to 360
- slopes: float32 [64], P('head'), may hold values from 3.6621094e-05 to 0.06, as said below
- doc_lengths: int32 [8], replicated, may hold values from 1 to 4096, 8192 in all
- norm_gain: float32 [8192], P('head'), may hold values from 0.1 to 1.9
Outputs:
- attended: bfloat16 [8192, 8192], P('seq', 'head')
Inputs may be any that keep to these rules, and one draw needn't show every extreme that they name: `slopes`: each head's rate lies between 0.3 / 8192 and 0.06.
All inputs are finite; a program needn't handle non-finite values.
Results may differ from a plain program's by a relative error of at most 0.0056.
Values may be sent and summed in bfloat16 or wider, within the bound.
A program may use at most 128 MiB of HBM per device.

v0:
```python
import jax
import jax.numpy as jnp
from jax import lax
from jax.sharding import PartitionSpec as P

H = 64
DH = 128
BLOCK = 256


def carried_in(x, axis, combine, identity):
    count, place = (lax.axis_size(axis), lax.axis_index(axis))
    everything = jax.tree.map(lambda part: lax.all_gather(part, axis), x)
    start = jax.tree.map(
        lambda part, zero: jnp.broadcast_to(jnp.asarray(zero, part.dtype), part.shape), x, identity
    )

    def turn(k, before):
        reached = k < place
        new = combine(before, jax.tree.map(lambda part: part[k], everything))
        return jax.tree.map(lambda a, b: jnp.where(reached, a, b), new, before)

    return lax.fori_loop(0, count, turn, start)


def segment_of(positions, doc_lengths):
    starts = jnp.cumsum(doc_lengths) - doc_lengths
    later_starts = starts[1:]
    counted = jnp.sum((positions[..., None] >= later_starts).astype(jnp.int32), axis=-1)
    return jnp.where(positions < 0, -1, counted)


def head_linker(earlier, later_pair):
    return (earlier[0] * later_pair[0], later_pair[0][..., None] * earlier[1] + later_pair[1])


def shards(queries, key_rows, values, slopes, doc_lengths, norm_gain):
    tok_rows, feat_cols = queries.shape
    heads_local = slopes.shape[0]
    head_size = feat_cols // heads_local
    blocks = tok_rows // BLOCK
    seq_rank = lax.axis_index("seq")
    offsets = jnp.arange(BLOCK, dtype=jnp.int32)
    positions = seq_rank * tok_rows + jnp.arange(tok_rows, dtype=jnp.int32).reshape(blocks, BLOCK)
    segment = segment_of(positions, doc_lengths)
    before = segment_of(positions[:, 0] - 1, doc_lengths)
    query_blocks = queries.reshape(blocks, BLOCK, heads_local, head_size)
    key_blocks = key_rows.reshape(blocks, BLOCK, heads_local, head_size)
    value_blocks = values.reshape(blocks, BLOCK, heads_local, head_size)
    lags = offsets[:, None] - offsets[None, :]
    distance = jnp.maximum(lags, 0).astype(jnp.float32)
    allowed = (lags >= 0)[None] & (segment[:, :, None] == segment[:, None, :])
    decay_mask = jnp.where(
        allowed[:, None], jnp.exp(-slopes[None, :, None, None] * distance[None, None]), 0.0
    )
    scores = jnp.einsum(
        "cthd,cshd->chts", query_blocks, key_blocks, preferred_element_type=jnp.float32
    )
    weights = (scores * decay_mask).astype(jnp.bfloat16)
    intra_part = jnp.einsum(
        "chts,cshd->cthd", weights, value_blocks, preferred_element_type=jnp.float32
    )
    remaining = (BLOCK - 1 - offsets).astype(jnp.float32)
    scale_rows = jnp.where(
        (segment == segment[:, -1:])[:, :, None],
        jnp.exp(-slopes[None, None, :] * remaining[None, :, None]),
        0.0,
    )
    weighted = (scale_rows[..., None] * value_blocks).astype(jnp.bfloat16)
    local_states = jnp.einsum(
        "cshd,cshe->chde", key_blocks, weighted, preferred_element_type=jnp.float32
    )
    local_factors = jnp.where(
        (before == segment[:, -1])[:, None], jnp.exp(-slopes * BLOCK)[None, :], 0.0
    )
    state_rows = local_states.reshape(blocks, heads_local, head_size * head_size)
    running_factor, running_state = lax.associative_scan(
        head_linker, (local_factors, state_rows), axis=0
    )
    identity = (
        jnp.ones((heads_local,), jnp.float32),
        jnp.zeros((heads_local, head_size * head_size), jnp.float32),
    )
    carried = carried_in((running_factor[-1], running_state[-1]), "seq", head_linker, identity)
    carry_state = carried[1]
    state_ends = running_factor[..., None] * carry_state[None] + running_state
    entering_all = jnp.concatenate([carry_state[None], state_ends[:-1]], axis=0).astype(
        jnp.bfloat16
    )
    entering = entering_all.reshape(blocks, heads_local, head_size, head_size)
    reach = (offsets + 1).astype(jnp.float32)
    carry_rows = jnp.where(
        (segment == before[:, None])[:, :, None],
        jnp.exp(-slopes[None, None, :] * reach[None, :, None]),
        0.0,
    )
    inter_part = (
        jnp.einsum("cthd,chde->cthe", query_blocks, entering, preferred_element_type=jnp.float32)
        * carry_rows[..., None]
    )
    mixed_out = (intra_part + inter_part).reshape(tok_rows, feat_cols)
    squares = lax.psum(jnp.sum(mixed_out * mixed_out, axis=1), "head")
    inverse = lax.rsqrt(squares / (H * DH) + 1e-05)
    return (mixed_out * inverse[:, None] * norm_gain[None, :]).astype(jnp.bfloat16)


def solution(mesh):
    placed = (P("seq", "head"), P("seq", "head"), P("seq", "head"), P("head"), P(), P("head"))
    return jax.shard_map(
        shards, mesh=mesh, in_specs=placed, out_specs=P("seq", "head"), check_vma=False
    )
```

profile of v0, /device:TPU:24, one launch (start us, length us, event | category | flops | bytes accessed | tf_op | source)
XLA Modules:
  0.0 318.0 jit_solution(929701023700362041)
XLA Ops:
  9.9 5.5 %copy.78 = bf16[64,8,32,128]{3,2,1,0:T(8,128)(2,1)} copy(bf16[64,8,32,128]{3,1,2,0:T(8,128)(2,1)} %bitcast.67) | data formatting | bytes 8388608
  15.4 7.5 %copy.66 = bf16[2,256,32,128]{1,3,2,0:T(8,128)(2,1)} copy(bf16[2,256,32,128]{3,2,1,0:T(8,128)(2,1)} %bitcast.64) | data formatting | bytes 8388608 | tf_op jit(solution)/shard_map/reshape | solution.py:49
  22.9 3.6 %copy.79 = bf16[64,8,32,128]{3,2,1,0:T(8,128)(2,1)S(1)} copy(bf16[64,8,32,128]{3,1,2,0:T(8,128)(2,1)} %bitcast.68) | data formatting | bytes 8388608
  26.6 2.9 fusion.21
  29.6 2.5 fusion.36
  34.1 3.6 %copy.71 = f32[1,32,128,128]{3,2,0,1:T(8,128)} copy(f32[1,32,128,128]{2,3,1,0:T(8,128)} %get-tuple-element.136) | data formatting | bytes 4194304 | tf_op jit(solution)/shard_map/slice | solution.py:77
  37.8 4.9 %multiply_add_fusion = f32[1,32,16384]{2,0,1:T(1,128)S(1)} fusion(f32[1,32,16384]{2,0,1:T(1,128)} %bitcast.65, f32[1,32,16384]{2,0,1:T(1,128)S(1)} %bitcast.60, f32[32]{0:T(128)S(1)} %get-tuple-element.140), kind=kLoop, calls=%fused_computation.34 | loop fusion | flops 1048576 | bytes 6291584 | tf_op jit(solution)/shard_map/add | solution.py:34
  42.7 3.5 %fusion.24 = f32[1,32,16384]{2,0,1:T(1,128)S(1)} fusion(f32[1,32,16384]{2,0,1:T(1,128)S(1)} %bitcast.61, f32[1,32,16384]{2,0,1:T(1,128)S(1)} %multiply_add_fusion), kind=kLoop, calls=%fused_computation.27 | loop fusion | flops 524288 | bytes 6291456 | tf_op jit(solution)/shard_map/add | solution.py:77
  46.2 2.6 copy.72
  48.9 5.5 %copy.80 = bf16[64,8,32,128]{3,2,1,0:T(8,128)(2,1)} copy(bf16[64,8,32,128]{3,1,2,0:T(8,128)(2,1)} %bitcast.69) | data formatting | bytes 8388608
  54.4 17.5 %all-gather = f32[16,1,32]{2,1,0:T(1,128)S(1)} all-gather(f32[1,1,32]{2,1,0:T(1,128)S(1)} %get-tuple-element.138), channel_id=1, replica_groups=mesh['seq'=16,'head'=2] {'seq'}, dimensions={0}, use_global_device_ids=true | all-gather | bytes 2176 | tf_op jit(solution)/shard_map/all_gather | solution.py:13
  72.1 4.3 %multiply_exponential_fusion = f32[32,256,256]{2,1,0:T(8,128)} fusion(f32[256,256]{1,0:T(8,128)S(1)} %maximum_convert_fusion, f32[32]{0:T(128)S(1)} %get-tuple-element.143), kind=kLoop, calls=%fused_computation.14 | loop fusion | flops 2097152 | bytes 8650880 | tf_op jit(solution)/shard_map/exp | solution.py:54
  76.5 12.8 %fusion.1 = f32[2,32,256,128]{2,3,1,0:T(8,128)} fusion(bf16[2,256,32,128]{1,3,2,0:T(8,128)(2,1)} %copy.66, f32[32,256,256]{2,1,0:T(8,128)} %multiply_exponential_fusion, pred[2,256,256]{2,1,0:T(8,128)(4,1)S(1)} %compare_and_fusion, bf16[2,256,32,128]{3,2,1,0:T(8,128)(2,1)} %bitcast.57, bf16[2,256,32,128]{3,2,1,0:T(8,128)(2,1)} %bitcast.58), kind=kOutput, calls=%fused_computation.4 | convolution fusion | flops 2160066560 | bytes 29491200 | tf_op jit(solution)/shard_map/chts,cshd->cthd/dot_general | solution.py:60
  89.3 128.7 %all-gather.3.cloned.1.call-done = f32[16,32,16384]{2,1,0:T(8,128)} async-done(((f32[1,32,16384]{2,1,0:T(8,128)}), f32[16,32,16384]{2,1,0:T(8,128)}) %all-gather.3.cloned.1.call-update) | async-done | bytes 33554448 | tf_op jit(solution)/shard_map/all_gather | solution.py:13
  218.0 41.0 %while.14 = (s32[]{:T(128)}, f32[32,16384]{1,0:T(8,128)S(1)}, s32[]{:T(128)}, f32[16,32]{1,0:T(8,128)S(1)}, f32[16,32,16384]{2,1,0:T(8,128)}, /*index=5*/s32[]{:T(128)}, s32[]{:T(128)}) while((s32[]{:T(128)}, f32[32,16384]{1,0:T(8,128)S(1)}, s32[]{:T(128)}, f32[16,32]{1,0:T(8,128)S(1)}, f32[16,32,16384]{2,1,0:T(8,128)}, ...), condition=%wide.region_4.5_spmd.clone, body=%wide.region_3.4_spmd.clone.sunk | while | flops 2097156 | bytes 6291945 | solution.py:23
  223.1 2.5 fusion.40
  225.7 2.5 fusion.40
  228.3 2.5 fusion.40
  230.8 2.5 fusion.40
  260.7 9.2 %convert_reduce_fusion = bf16[32,16384]{1,0:T(8,128)(2,1)S(1)} fusion(f32[1,32,16384]{2,0,1:T(1,128)} %copy-done.4, f32[1,32,16384]{2,0,1:T(1,128)S(1)} %bitcast.62, f32[32,16384]{1,0:T(8,128)S(1)} %get-tuple-element.99, f32[1,32]{0,1:T(8,128)S(1)} %copy.100), kind=kLoop, calls=%fused_computation.33 | loop fusion | flops 2097152 | bytes 7340160 | tf_op jit(solution)/shard_map/slice | solution.py:87
  273.7 10.7 %multiply_reduce_fusion = (f32[2,256]{1,0:T(2,128)S(1)}, f32[2,256,32,128]{1,3,2,0:T(8,128)}) fusion(f32[2,256,32]{1,2,0:T(8,128)S(1)} %get-tuple-element.148, bf16[2,256,32,128]{3,2,1,0:T(8,128)(2,1)} %bitcast.59, bf16[1,32,128,128]{2,3,1,0:T(8,128)(2,1)S(1)} %copy.75, bf16[1,32,128,128]{2,3,1,0:T(8,128)(2,1)S(1)} %copy.74, f32[2,32,256,128]{2,3,1,0:T(8,128)} %fusion.1), kind=kOutput, calls=%fused_computation.10 | convolution fusion | flops 546307584 | bytes 23136256 | tf_op jit(solution)/shard_map/cthd,chde->cthe/dot_general | solution.py:98
  284.4 10.3 %copy.77 = f32[2,256,32,128]{3,2,1,0:T(8,128)} copy(f32[2,256,32,128]{1,3,2,0:T(8,128)} %get-tuple-element.147) | data formatting | bytes 16777216 | tf_op jit(solution)/shard_map/add | solution.py:101
  294.7 5.1 %psum.7 = f32[512]{0:T(512)S(1)} all-reduce(f32[512]{0:T(512)S(1)} %bitcast.74), channel_id=1, replica_groups=mesh['seq'=16,'head'=2] {'head'}, use_global_device_ids=true, to_apply=%region_6.7 | all-reduce | flops 512 | bytes 4096 | tf_op jit(solution)/shard_map/psum | solution.py:102
  299.8 11.3 %fusion.3 = bf16[512,4096]{1,0:T(8,128)(2,1)} fusion(f32[64,8,32,128]{3,2,1,0:T(8,128)} %bitcast.63, f32[4096]{0:T(1024)S(1)} %copy-done.5, f32[512]{0:T(512)S(1)} %add_rsqrt_fusion), kind=kLoop, calls=%fused_computation.7 | loop fusion | flops 6291456 | bytes 12601344 | tf_op jit(solution)/shard_map/convert_element_type | solution.py:104
  (77 shorter events, 41.6 us)
Async XLA Ops:
  6.5 211.5 %all-gather.3.cloned.1.call-start = ((), (), s32[]{:S(2)}) async-start(), calls=%async_computation | async-start | bytes 35651584 | tf_op jit(solution)/shard_map/all_gather | solution.py:13
  22.9 3.7 %copy-start = (bf16[2,256,32,128]{1,3,2,0:T(8,128)(2,1)S(1)}, bf16[2,256,32,128]{1,3,2,0:T(8,128)(2,1)}, u32[]{:S(2)}) copy-start(bf16[2,256,32,128]{1,3,2,0:T(8,128)(2,1)} %copy.66) | copy-start | bytes 12582916
  26.5 3.1 copy-start.1
  34.0 8.6 %copy-start.2 = (f32[1,32,128,128]{3,2,0,1:T(8,128)}, f32[1,32,128,128]{3,2,0,1:T(8,128)S(1)}, u32[]{:S(2)}) copy-start(f32[1,32,128,128]{3,2,0,1:T(8,128)S(1)} %copy.70) | copy-start | bytes 6291460
  42.7 3.5 %copy-start.4 = (f32[1,32,16384]{2,0,1:T(1,128)}, f32[1,32,16384]{2,0,1:T(1,128)S(1)}, u32[]{:S(2)}) copy-start(f32[1,32,16384]{2,0,1:T(1,128)S(1)} %multiply_add_fusion) | copy-start | bytes 6291460
  259.1 1.6 copy-start.3
  284.4 15.4 %copy-start.5 = (f32[4096]{0:T(1024)S(1)}, f32[4096]{0:T(1024)}, u32[]{:S(2)}) copy-start(f32[4096]{0:T(1024)} %param.13) | copy-start | bytes 49156
Sparse Core Ops, SparseCore 0:
  48.9 169.0 all-gather.2
where the time goes:
time: 321 us; the launch traced here: 318 us
  waiting for transfers between devices  129 us (40%)
  other arithmetic  77.2 us (24%)
  local copies, waits for them, and re-layouts  48.8 us (15%)
  matrix products  26.5 us (8%)
  blocking collectives  22.6 us (7%)
  between operations  13.6 us (4%)
    all_gather x1, waiting for transfers between devices, carried_in(): everything = jax.tree.map(lambda part: lax.all_gather(part, axis), x)  129 us
    select_n x16, other arithmetic, turn(): return jax.tree.map(lambda a, b: jnp.where(reached, a, b), new, before)  40.4 us
    unnamed x19, local copies, waits for them, and re-layouts  17.5 us
    all_gather x1, blocking collectives, carried_in(): everything = jax.tree.map(lambda part: lax.all_gather(part, axis), x)  17.5 us
    dot_general x1, matrix products, shards(): jnp.einsum('chts,cshd->cthd', weights, value_blocks, preferred_element_ty...  12.8 us
    convert_element_type x1, other arithmetic, shards(): (mixed_out * inverse[:, None] * norm_gain[None, :]).astype(jnp.bfloat16)  11.3 us
    dot_general x1, matrix products, shards(): jnp.einsum('cthd,chde->cthe', query_blocks, entering, preferred_element_t...  10.7 us
    add x1, local copies, waits for them, and re-layouts, shards(): mixed_out = (intra_part + inter_part).reshape(tok_rows, feat_cols)  10.3 us
  transfers between devices with their start and end apart: 1, of which 1 were waited for; matrix products, arithmetic and copies ran while one was open for 7% of the time, Pallas kernels for 0%

commit v1 on v0

v1 whole, which is shorter than its diff:
```python
import functools

import jax
import jax.numpy as jnp
from jax import lax
from jax.experimental import pallas as pl
from jax.experimental.pallas import tpu as pltpu
from jax.sharding import PartitionSpec as P

BLOCK = 256
FAR = 1e30
F32 = jnp.float32
BF16 = jnp.bfloat16
MESH = pl.DeviceIdType.MESH


def kernel(
    planes, head_parts, heads, blocks, parts,
    slopes_ref, docs_ref, q_hbm, k_hbm, v_hbm,
    mixed_hbm, inv_ref,
    q_ref, k_ref, v_ref, mixed_ref, out_ref, local_ref, own_ref, carry_ref,
    s_send, s_recv, p_send, p_recv, x_recv, c_send, c_recv,
    lag_ref, same_ref, tail_ref, lead_ref, rem_ref, reach_ref, sq_ref, sq_send, sq_recv,
    q_sem, k_sem, v_sem, o_sem,
    s_out, s_in, p_out, p_in, x_out, x_in, c_out, c_in, sq_out, sq_in,
):
    half = heads // 2
    step = half // parts
    chunks = 2 * parts
    rows = blocks * BLOCK
    size = q_ref.shape[1] // heads
    seq = lax.axis_index("seq")
    headpos = lax.axis_index("head")
    core = lax.rem(seq, 2)
    side = lax.rem(lax.div(seq, 2), 2)
    plane = lax.div(seq, 4)
    partner = seq + 1 - 2 * core
    across = seq + 2 - 4 * side
    ahead = jnp.minimum(seq + 4, 4 * planes - 1)
    first = (1 - core) * half

    def head_of(o):
        return lax.rem(o + first, heads)

    def cols(h):
        return pl.ds(pl.multiple_of(h * size, size), size)

    def wide(oc):
        return pl.ds(pl.multiple_of(head_of(oc * step) * size, step * size), step * size)

    def load(hbm, ref, sem, oc):
        return pltpu.make_async_copy(hbm.at[:, wide(oc)], ref.at[:, wide(oc)], sem.at[oc])

    def store(oc):
        return pltpu.make_async_copy(out_ref.at[:, wide(oc)], mixed_hbm.at[:, wide(oc)], o_sem.at[oc])

    def piece(c):
        return pl.ds(c * step, step)

    def remote(src, dst, c, out_sem, in_sem, target):
        return pltpu.make_async_remote_copy(
            src_ref=src.at[piece(c)], dst_ref=dst.at[piece(c)],
            send_sem=out_sem.at[c], recv_sem=in_sem.at[c],
            device_id={"seq": target}, device_id_type=MESH,
        )

    def s_copy(c):
        return remote(s_send, s_recv, c, s_out, s_in, partner)

    def p_copy(c):
        return remote(p_send, p_recv, c, p_out, p_in, ahead)

    def x_copy(c, src):
        return remote(src, x_recv, c, x_out, x_in, across)

    def c_copy(c):
        return remote(c_send, c_recv, c, c_out, c_in, partner)

    def each(count, body, start=0):
        def turn(i, _):
            body(i)
            return 0
        lax.fori_loop(start, count, turn, 0)

    barrier = pltpu.get_barrier_semaphore()
    pl.semaphore_signal(barrier, inc=1, device_id={"seq": partner}, device_id_type=MESH)
    pl.semaphore_signal(barrier, inc=1, device_id={"seq": across}, device_id_type=MESH)

    @pl.when(plane < planes - 1)
    def _():
        pl.semaphore_signal(barrier, inc=1, device_id={"seq": seq + 4}, device_id_type=MESH)

    @pl.when(plane > 0)
    def _():
        pl.semaphore_signal(barrier, inc=1, device_id={"seq": seq - 4}, device_id_type=MESH)

    for i in range(1, head_parts):
        pl.semaphore_signal(
            barrier, inc=1, device_id={"head": lax.rem(headpos + i, head_parts)}, device_id_type=MESH
        )

    def begin_kv(oc):
        load(k_hbm, k_ref, k_sem, oc).start()
        load(v_hbm, v_ref, v_sem, oc).start()

    each(chunks, begin_kv)
    each(chunks, lambda oc: load(q_hbm, q_ref, q_sem, oc).start())

    starts = []
    total = jnp.int32(0)
    for j in range(docs_ref.shape[0] - 1):
        total = total + docs_ref[j]
        starts.append(total)

    def segment(pos):
        counted = jnp.zeros_like(pos)
        for s in starts:
            counted = counted + jnp.where(pos >= s, 1, 0)
        return jnp.where(pos < 0, -1, counted)

    def joined(a, b):
        return jnp.where(segment(a) == segment(b), F32(1), F32(0))

    base = seq * rows
    chip = base - core * rows
    down = lax.broadcasted_iota(jnp.int32, (BLOCK, BLOCK), 0)
    along = lax.broadcasted_iota(jnp.int32, (BLOCK, BLOCK), 1)
    lag_ref[...] = jnp.where(down >= along, (down - along).astype(F32), F32(FAR))
    offs = lax.broadcasted_iota(jnp.int32, (BLOCK, size), 0)
    rem_ref[...] = (BLOCK - 1 - offs).astype(F32)
    reach_ref[...] = (offs + 1).astype(F32)
    within = []
    for b in range(blocks):
        b0 = base + b * BLOCK
        row_seg = segment(b0 + offs)
        same_ref[b] = jnp.where(segment(b0 + down) == segment(b0 + along), F32(1), F32(0))
        tail_ref[b] = jnp.where(row_seg == segment(b0 + BLOCK - 1), F32(1), F32(0))
        lead_ref[b] = jnp.where(row_seg == segment(b0 - 1), F32(1), F32(0))
        within.append(joined(b0 - 1, b0 + BLOCK - 1))
    j_cores = joined(chip + rows - 1, chip + 2 * rows - 1)
    j_first = joined(chip - 1, chip + rows - 1)
    j_chain = joined(chip - 2 * rows - 1, chip + 2 * rows - 1)
    j_skip = joined(chip - 2 * rows - 1, chip - 1)

    def fade(h, distance, keep):
        return jnp.exp(jnp.full((1, size), -slopes_ref[h] * distance, F32)) * keep

    sq_ref[...] = jnp.zeros_like(sq_ref)

    @pl.when(plane == 0)
    def _():
        p_recv[...] = jnp.zeros_like(p_recv)

    def end_state(h):
        r = slopes_ref[h]
        scale = jnp.exp(rem_ref[...] * (-r))
        state = None
        for b in range(blocks):
            here = pl.ds(b * BLOCK, BLOCK)
            weighted = (scale * tail_ref[b] * v_ref[here, cols(h)].astype(F32)).astype(BF16)
            one = lax.dot_general(
                k_ref[here, cols(h)], weighted, (((0,), (0,)), ((), ())), preferred_element_type=F32
            )
            if b < blocks - 1:
                local_ref[b, h] = one
            state = one if state is None else fade(h, F32(BLOCK), within[b]) * state + one
        return state

    def wait_kv(oc):
        load(k_hbm, k_ref, k_sem, oc).wait()
        load(v_hbm, v_ref, v_sem, oc).wait()

    def give(i):
        s_send[i] = end_state(first + i).astype(BF16)

    def keep(i):
        own_ref[i] = end_state(core * half + i)

    def first_chunk(c):
        wait_kv(c)
        each((c + 1) * step, give, c * step)

    first_chunk(jnp.int32(0))
    beside = jnp.where(plane > 0, 1, 0) + jnp.where(plane < planes - 1, 1, 0)
    pl.semaphore_wait(barrier, 1 + head_parts + beside)
    s_copy(0).start()

    def next_chunk(c):
        first_chunk(c)
        s_copy(c).start()

    each(parts, next_chunk, 1)

    def own_chunk(c):
        wait_kv(parts + c)
        each((c + 1) * step, keep, c * step)

    each(parts, own_chunk)

    def intra(h):
        decay = jnp.exp(lag_ref[...] * (-slopes_ref[h]))
        for b in range(blocks):
            here = pl.ds(b * BLOCK, BLOCK)
            scores = lax.dot_general(
                q_ref[here, cols(h)], k_ref[here, cols(h)], (((1,), (1,)), ((), ())),
                preferred_element_type=F32,
            )
            weights = (scores * decay * same_ref[b]).astype(BF16)
            mixed_ref[here, cols(h)] = jnp.dot(
                weights, v_ref[here, cols(h)], preferred_element_type=F32
            )

    def intra_chunk(oc):
        load(q_hbm, q_ref, q_sem, oc).wait()
        each((oc + 1) * step, lambda o: intra(head_of(o)), oc * step)

    is_second = core == 1

    def chip_states(i):
        mine, other = own_ref[i], s_recv[i].astype(F32)
        return jnp.where(is_second, other, mine), jnp.where(is_second, mine, other)

    def chain(i):
        h = core * half + i
        early, late = chip_states(i)
        chip_state = fade(h, F32(rows), j_cores) * early + late
        p_send[i] = (fade(h, F32(4 * rows), j_chain) * p_recv[i].astype(F32) + chip_state).astype(BF16)

    def chain_chunk(c):
        s_copy(c).wait_recv()

        @pl.when(plane > 0)
        def _():
            p_copy(c).wait_recv()

        @pl.when(side == 1)
        def _():
            x_copy(c, p_recv).start()

        each((c + 1) * step, chain, c * step)

        @pl.when(plane < planes - 1)
        def _():
            p_copy(c).start()

        @pl.when(side == 0)
        def _():
            x_copy(c, p_send).start()

    head_start = jnp.minimum(plane, parts)
    each(head_start, intra_chunk)

    def chain_and_intra(c):
        chain_chunk(c)
        intra_chunk(head_start + c)

    each(parts, chain_and_intra)
    each(chunks, intra_chunk, head_start + parts)

    def settle(i):
        h = core * half + i
        early, _ = chip_states(i)
        enters = fade(h, F32(2 * rows), j_skip) * p_recv[i].astype(F32) + x_recv[i].astype(F32)
        second = fade(h, F32(rows), j_first) * enters + early
        carry_ref[i] = jnp.where(is_second, second, enters)
        c_send[i] = jnp.where(is_second, enters, second).astype(BF16)

    def finish(h, enters):
        reach = jnp.exp(reach_ref[...] * (-slopes_ref[h]))
        for b in range(blocks):
            here = pl.ds(b * BLOCK, BLOCK)
            inter = jnp.dot(q_ref[here, cols(h)], enters.astype(BF16), preferred_element_type=F32)
            mixed = mixed_ref[here, cols(h)] + inter * (reach * lead_ref[b])
            sq_ref[here, :] += mixed * mixed
            out_ref[here, cols(h)] = mixed.astype(BF16)
            if b < blocks - 1:
                enters = fade(h, F32(BLOCK), within[b]) * enters + local_ref[b, h]

    def settle_chunk(c):
        x_copy(c, p_recv).wait_recv()
        each((c + 1) * step, settle, c * step)
        c_copy(c).start()
        each((c + 1) * step, lambda i: finish(core * half + i, carry_ref[i]), c * step)
        store(parts + c).start()

    each(parts, settle_chunk)

    def last_chunk(c):
        c_copy(c).wait_recv()
        each((c + 1) * step, lambda i: finish(first + i, c_recv[i].astype(F32)), c * step)
        store(c).start()

    each(parts, last_chunk)

    ones = jnp.ones((8, size), F32)
    summed = lax.dot_general(
        ones, sq_ref[...], (((1,), (1,)), ((), ())),
        precision=lax.Precision.HIGHEST, preferred_element_type=F32,
    )
    sq_send[...] = summed

    def sq_copy(i):
        return pltpu.make_async_remote_copy(
            src_ref=sq_send, dst_ref=sq_recv.at[i], send_sem=sq_out.at[i], recv_sem=sq_in.at[i],
            device_id={"head": lax.rem(headpos + i, head_parts)}, device_id_type=MESH,
        )

    for i in range(1, head_parts):
        sq_copy(i).start()

    def drain(c):
        s_copy(c).wait_send()
        x_copy(c, p_send).wait_send()
        c_copy(c).wait_send()

        @pl.when(plane < planes - 1)
        def _():
            p_copy(c).wait_send()

    each(parts, drain)
    for i in range(1, head_parts):
        sq_copy(i).wait_recv()
        summed = summed + sq_recv[i]
    inverse = lax.rsqrt(summed / F32(heads * size * head_parts) + F32(1e-05))
    inv_ref[...] = jnp.broadcast_to(jnp.transpose(inverse)[:, 0:1], inv_ref.shape)
    for i in range(1, head_parts):
        sq_copy(i).wait_send()
    each(chunks, lambda oc: store(oc).wait())


def shards(planes, head_parts, queries, key_rows, values, slopes, doc_lengths, norm_gain):
    rows, feat = queries.shape
    heads = slopes.shape[0]
    size = feat // heads
    blocks = rows // BLOCK
    half = heads // 2
    parts = min(4, half)
    hbm = pl.BlockSpec(memory_space=pl.ANY)
    smem = pl.BlockSpec(memory_space=pltpu.SMEM)
    states = lambda dtype: pltpu.VMEM((half, size, size), dtype)
    dma = lambda n: pltpu.SemaphoreType.DMA((n,))
    mixed, inverse = pl.pallas_call(
        functools.partial(kernel, planes, head_parts, heads, blocks, parts),
        out_shape=(
            jax.ShapeDtypeStruct((rows, feat), BF16),
            jax.ShapeDtypeStruct((rows, size), F32),
        ),
        in_specs=[smem, smem, hbm, hbm, hbm],
        out_specs=(hbm, pl.BlockSpec(memory_space=pltpu.VMEM)),
        scratch_shapes=[
            pltpu.VMEM((rows, feat), BF16),
            pltpu.VMEM((rows, feat), BF16),
            pltpu.VMEM((rows, feat), BF16),
            pltpu.VMEM((rows, feat), F32),
            pltpu.VMEM((rows, feat), BF16),
            pltpu.VMEM((max(blocks - 1, 1), heads, size, size), F32),
            states(F32),
            states(F32),
            *[states(BF16)] * 7,
            pltpu.VMEM((BLOCK, BLOCK), F32),
            pltpu.VMEM((blocks, BLOCK, BLOCK), F32),
            pltpu.VMEM((blocks, BLOCK, size), F32),
            pltpu.VMEM((blocks, BLOCK, size), F32),
            pltpu.VMEM((BLOCK, size), F32),
            pltpu.VMEM((BLOCK, size), F32),
            pltpu.VMEM((rows, size), F32),
            pltpu.VMEM((8, rows), F32),
            pltpu.VMEM((head_parts, 8, rows), F32),
            *[dma(2 * parts)] * 4,
            *[dma(parts)] * 8,
            dma(head_parts),
            dma(head_parts),
        ],
        compiler_params=pltpu.CompilerParams(
            collective_id=0, has_side_effects=True, vmem_limit_bytes=56 * 1024 * 1024
        ),
    )(slopes, doc_lengths, queries, key_rows, values)
    return (mixed.astype(F32) * inverse[:, :1] * norm_gain[None, :]).astype(BF16)


def solution(mesh):
    placed = (P("seq", "head"), P("seq", "head"), P("seq", "head"), P("head"), P(), P("head"))
    return jax.shard_map(
        functools.partial(shards, mesh.shape["seq"] // 4, mesh.shape["head"]),
        mesh=mesh, in_specs=placed, out_specs=P("seq", "head"), check_vma=False,
    )
```

time: 321 us -> 54.4 us (0.17)
  waiting for transfers between devices: 129 us -> 0 us
  other arithmetic: 77.2 us -> 5.84 us
  local copies, waits for them, and re-layouts: 48.8 us -> 1.09 us
  Pallas kernels: 0 us -> 47.2 us
  matrix products: 26.5 us -> 0 us
  blocking collectives: 22.6 us -> 0 us
  between operations: 13.6 us -> 0.02 us
    all_gather x1 -> x0, waiting for transfers between devices: 129 us -> none  [carried_in(): everything = jax.tree.map(lambda part: lax.all_gather(part, axis), x)]
    pallas_call x0 -> x1, Pallas kernels: none -> 47.2 us  [shards(): pl.pallas_call(functools.partial(kernel, planes, head_parts, heads, block...]
    select_n x19 -> x0, other arithmetic: 40.6 us -> none  [the longest x16 40.4 us: turn(): return jax.tree.map(lambda a, b: jnp.where(reached, a, b), new, before)]
    dot_general x3 -> x0, matrix products: 26.5 us -> none  [the longest x1 12.8 us: shards(): jnp.einsum('chts,cshd->cthd', weights, value_blocks, preferred_element_ty...]
    unnamed x19 -> x2, local copies, waits for them, and re-layouts: 17.5 us -> 0.01 us
    all_gather x1 -> x0, blocking collectives: 17.5 us -> none  [carried_in(): everything = jax.tree.map(lambda part: lax.all_gather(part, axis), x)]
    add x1 -> x0, local copies, waits for them, and re-layouts: 10.3 us -> none  [shards(): mixed_out = (intra_part + inter_part).reshape(tok_rows, feat_cols)]
    slice x7 -> x1, local copies, waits for them, and re-layouts: 10.9 us -> 1.09 us  [shards(): inverse[:, :1]]
  transfers between devices with their start and end apart: 1 -> 0, of which waited for: 1 -> 0; matrix products, arithmetic and copies ran while one was open for 7% -> 0% of each run, Pallas kernels for 0% -> 0%
where the time goes in v1:
time: 54.4 us; the launch traced here: 54.2 us
  Pallas kernels  47.2 us (87%)
  other arithmetic  5.84 us (11%)
  local copies, waits for them, and re-layouts  1.09 us (2%)
    pallas_call x1, Pallas kernels, shards(): pl.pallas_call(functools.partial(kernel, planes, head_parts, heads, block...  47.2 us
    convert_element_type x1, other arithmetic, shards(): (mixed.astype(F32) * inverse[:, :1] * norm_gain[None, :]).astype(BF16)  5.84 us
    slice x1, local copies, waits for them, and re-layouts, shards(): inverse[:, :1]  1.09 us

profile of v1, /device:TPU:24, one launch (start us, length us, event | category | flops | bytes accessed | tf_op | source)
XLA Modules:
  0.0 54.2 jit_solution(1570592582792056390)
XLA Ops:
  0.0 0.0 copy-start
  0.0 47.2 %shard_map.64 = (bf16[512,4096]{1,0:T(8,128)(2,1)}, f32[512,128]{1,0:T(8,128)}) custom-call(f32[32]{0:T(128)} %slopes_ref.1, s32[8]{0:T(128)} %docs_ref.1, bf16[512,4096]{1,0:T(8,128)(2,1)} %q_hbm.1, bf16[512,4096]{1,0:T(8,128)(2,1)} %k_hbm.1, bf16[512,4096]{1,0:T(8,128)(2,1)} %v_hbm.1), custom_call_target="tpu_custom_call" | custom-call | tf_op jit(solution)/shard_map/pallas_call | solution.py:342
  47.2 1.1 %slice_reduce_fusion = f32[512]{0:T(512)S(1)} fusion(f32[512,128]{1,0:T(8,128)} %get-tuple-element.8), kind=kLoop, calls=%fused_computation.1 | loop fusion | bytes 4096 | tf_op jit(solution)/shard_map/slice | solution.py:378
  48.3 0.0 copy-done
  48.3 5.8 %multiply_convert_fusion = bf16[512,4096]{1,0:T(8,128)(2,1)} fusion(bf16[512,4096]{1,0:T(8,128)(2,1)} %get-tuple-element.7, f32[4096]{0:T(1024)S(1)} %copy-done, f32[512]{0:T(512)S(1)} %slice_reduce_fusion), kind=kLoop, calls=%fused_computation | loop fusion | flops 8388608 | bytes 8407040 | tf_op jit(solution)/shard_map/convert_element_type | solution.py:378
Async XLA Ops:
  0.0 48.3 %copy-start = (f32[4096]{0:T(1024)S(1)}, f32[4096]{0:T(1024)}, u32[]{:S(2)}) copy-start(f32[4096]{0:T(1024)} %param.11) | copy-start | bytes 49156

commit v2 on v1

--- a/solution.py
+++ b/solution.py
@@ -9,6 +9,7 @@
 
 BLOCK = 256
 FAR = 1e30
+LOG2E = 1.4426950408889634
 F32 = jnp.float32
 BF16 = jnp.bfloat16
 MESH = pl.DeviceIdType.MESH
@@ -82,6 +83,10 @@
             return 0
         lax.fori_loop(start, count, turn, 0)
 
+    def grouped(c, body):
+        for i in range(step):
+            body(c * step + i)
+
     barrier = pltpu.get_barrier_semaphore()
     pl.semaphore_signal(barrier, inc=1, device_id={"seq": partner}, device_id_type=MESH)
     pl.semaphore_signal(barrier, inc=1, device_id={"seq": across}, device_id_type=MESH)
@@ -125,7 +130,8 @@
     chip = base - core * rows
     down = lax.broadcasted_iota(jnp.int32, (BLOCK, BLOCK), 0)
     along = lax.broadcasted_iota(jnp.int32, (BLOCK, BLOCK), 1)
-    lag_ref[...] = jnp.where(down >= along, (down - along).astype(F32), F32(FAR))
+    lag = jnp.where(down >= along, (down - along).astype(F32), F32(FAR))
+    lag_ref[...] = lag[BLOCK // 2:]
     offs = lax.broadcasted_iota(jnp.int32, (BLOCK, size), 0)
     rem_ref[...] = (BLOCK - 1 - offs).astype(F32)
     reach_ref[...] = (offs + 1).astype(F32)
@@ -142,8 +148,11 @@
     j_chain = joined(chip - 2 * rows - 1, chip + 2 * rows - 1)
     j_skip = joined(chip - 2 * rows - 1, chip - 1)
 
+    def rate(h):
+        return slopes_ref[h] * F32(-LOG2E)
+
     def fade(h, distance, keep):
-        return jnp.exp(jnp.full((1, size), -slopes_ref[h] * distance, F32)) * keep
+        return jnp.exp2(jnp.full((1, size), rate(h) * distance, F32)) * keep
 
     sq_ref[...] = jnp.zeros_like(sq_ref)
 
@@ -152,8 +161,7 @@
         p_recv[...] = jnp.zeros_like(p_recv)
 
     def end_state(h):
-        r = slopes_ref[h]
-        scale = jnp.exp(rem_ref[...] * (-r))
+        scale = jnp.exp2(rem_ref[...] * rate(h))
         state = None
         for b in range(blocks):
             here = pl.ds(b * BLOCK, BLOCK)
@@ -178,7 +186,7 @@
 
     def first_chunk(c):
         wait_kv(c)
-        each((c + 1) * step, give, c * step)
+        grouped(c, give)
 
     first_chunk(jnp.int32(0))
     beside = jnp.where(plane > 0, 1, 0) + jnp.where(plane < planes - 1, 1, 0)
@@ -193,26 +201,32 @@
 
     def own_chunk(c):
         wait_kv(parts + c)
-        each((c + 1) * step, keep, c * step)
+        grouped(c, keep)
 
     each(parts, own_chunk)
 
+    mid = BLOCK // 2
+
     def intra(h):
-        decay = jnp.exp(lag_ref[...] * (-slopes_ref[h]))
+        decay = jnp.exp2(lag_ref[...] * rate(h))
         for b in range(blocks):
             here = pl.ds(b * BLOCK, BLOCK)
             scores = lax.dot_general(
                 q_ref[here, cols(h)], k_ref[here, cols(h)], (((1,), (1,)), ((), ())),
                 preferred_element_type=F32,
             )
-            weights = (scores * decay * same_ref[b]).astype(BF16)
+            upper = (scores[:mid, :mid] * decay[:, mid:] * same_ref[b, :mid, :mid]).astype(BF16)
+            lower = (scores[mid:] * decay * same_ref[b, mid:, :]).astype(BF16)
+            weights = jnp.concatenate(
+                [jnp.concatenate([upper, jnp.zeros((mid, mid), BF16)], axis=1), lower], axis=0
+            )
             mixed_ref[here, cols(h)] = jnp.dot(
                 weights, v_ref[here, cols(h)], preferred_element_type=F32
             )
 
     def intra_chunk(oc):
         load(q_hbm, q_ref, q_sem, oc).wait()
-        each((oc + 1) * step, lambda o: intra(head_of(o)), oc * step)
+        grouped(oc, lambda o: intra(head_of(o)))
 
     is_second = core == 1
 
@@ -237,7 +251,7 @@
         def _():
             x_copy(c, p_recv).start()
 
-        each((c + 1) * step, chain, c * step)
+        grouped(c, chain)
 
         @pl.when(plane < planes - 1)
         def _():
@@ -265,29 +279,35 @@
         carry_ref[i] = jnp.where(is_second, second, enters)
         c_send[i] = jnp.where(is_second, enters, second).astype(BF16)
 
-    def finish(h, enters):
-        reach = jnp.exp(reach_ref[...] * (-slopes_ref[h]))
+    def finish_all(work):
+        fades = [jnp.exp2(reach_ref[...] * rate(h)) for h, _ in work]
+        states = [enters for _, enters in work]
         for b in range(blocks):
             here = pl.ds(b * BLOCK, BLOCK)
-            inter = jnp.dot(q_ref[here, cols(h)], enters.astype(BF16), preferred_element_type=F32)
-            mixed = mixed_ref[here, cols(h)] + inter * (reach * lead_ref[b])
-            sq_ref[here, :] += mixed * mixed
-            out_ref[here, cols(h)] = mixed.astype(BF16)
-            if b < blocks - 1:
-                enters = fade(h, F32(BLOCK), within[b]) * enters + local_ref[b, h]
+            squares = sq_ref[here, :]
+            for i, (h, _) in enumerate(work):
+                inter = jnp.dot(
+                    q_ref[here, cols(h)], states[i].astype(BF16), preferred_element_type=F32
+                )
+                mixed = mixed_ref[here, cols(h)] + inter * (fades[i] * lead_ref[b])
+                squares = squares + mixed * mixed
+                out_ref[here, cols(h)] = mixed.astype(BF16)
+                if b < blocks - 1:
+                    states[i] = fade(h, F32(BLOCK), within[b]) * states[i] + local_ref[b, h]
+            sq_ref[here, :] = squares
 
     def settle_chunk(c):
         x_copy(c, p_recv).wait_recv()
-        each((c + 1) * step, settle, c * step)
+        grouped(c, settle)
         c_copy(c).start()
-        each((c + 1) * step, lambda i: finish(core * half + i, carry_ref[i]), c * step)
+        finish_all([(core * half + c * step + i, carry_ref[c * step + i]) for i in range(step)])
         store(parts + c).start()
 
     each(parts, settle_chunk)
 
     def last_chunk(c):
         c_copy(c).wait_recv()
-        each((c + 1) * step, lambda i: finish(first + i, c_recv[i].astype(F32)), c * step)
+        finish_all([(first + c * step + i, c_recv[c * step + i].astype(F32)) for i in range(step)])
         store(c).start()
 
     each(parts, last_chunk)
@@ -326,6 +346,14 @@
     for i in range(1, head_parts):
         sq_copy(i).wait_send()
     each(chunks, lambda oc: store(oc).wait())
+
+
+def scale_kernel(mixed_ref, inv_ref, gain_ref, out_ref):
+    size = inv_ref.shape[1]
+    inverse = inv_ref[...]
+    for c in range(0, out_ref.shape[1], size):
+        piece = mixed_ref[:, c:c + size].astype(F32)
+        out_ref[:, c:c + size] = (piece * inverse * gain_ref[:, c:c + size]).astype(BF16)
 
 
 def shards(planes, head_parts, queries, key_rows, values, slopes, doc_lengths, norm_gain):
@@ -357,7 +385,7 @@
             states(F32),
             states(F32),
             *[states(BF16)] * 7,
-            pltpu.VMEM((BLOCK, BLOCK), F32),
+            pltpu.VMEM((BLOCK // 2, BLOCK), F32),
             pltpu.VMEM((blocks, BLOCK, BLOCK), F32),
             pltpu.VMEM((blocks, BLOCK, size), F32),
             pltpu.VMEM((blocks, BLOCK, size), F32),
@@ -375,7 +403,18 @@
             collective_id=0, has_side_effects=True, vmem_limit_bytes=56 * 1024 * 1024
         ),
     )(slopes, doc_lengths, queries, key_rows, values)
-    return (mixed.astype(F32) * inverse[:, :1] * norm_gain[None, :]).astype(BF16)
+    width = feat // 8
+    return pl.pallas_call(
+        scale_kernel,
+        out_shape=jax.ShapeDtypeStruct((rows, feat), BF16),
+        grid=(feat // width,),
+        in_specs=[
+            pl.BlockSpec((rows, width), lambda i: (0, i)),
+            pl.BlockSpec((rows, size), lambda i: (0, 0)),
+            pl.BlockSpec((1, width), lambda i: (0, i)),
+        ],
+        out_specs=pl.BlockSpec((rows, width), lambda i: (0, i)),
+    )(mixed, inverse, norm_gain.reshape(1, feat))
 
 
 def solution(mesh):

time: 54.4 us -> 48 us (0.88)
  other arithmetic: 5.84 us -> 0 us
  local copies, waits for them, and re-layouts: 1.09 us -> 0 us
    pallas_call x0 -> x1, Pallas kernels: none -> 7.1 us  [shards(): pl.pallas_call(scale_kernel, out_shape=jax.ShapeDtypeStruct((rows, feat),...]
    pallas_call x1, Pallas kernels: 47.2 us -> 40.6 us  [shards(): pl.pallas_call(functools.partial(kernel, planes, head_parts, heads, block...]
    convert_element_type x1 -> x0, other arithmetic: 5.84 us -> none  [shards(): (mixed.astype(F32) * inverse[:, :1] * norm_gain[None, :]).astype(BF16)]
    slice x1 -> x0, local copies, waits for them, and re-layouts: 1.09 us -> none  [shards(): inverse[:, :1]]
where the time goes in v2:
time: 48 us; the launch traced here: 47.7 us
  Pallas kernels  47.7 us (99%)
    pallas_call x1, Pallas kernels, shards(): pl.pallas_call(functools.partial(kernel, planes, head_parts, heads, block...  40.6 us
    pallas_call x1, Pallas kernels, shards(): pl.pallas_call(scale_kernel, out_shape=jax.ShapeDtypeStruct((rows, feat),...  7.1 us

profile of v2, /device:TPU:24, one launch (start us, length us, event | category | flops | bytes accessed | tf_op | source)
XLA Modules:
  0.0 47.7 jit_solution(8014292041274654436)
XLA Ops:
  0.0 40.6 %shard_map.64 = (bf16[512,4096]{1,0:T(8,128)(2,1)}, f32[512,128]{1,0:T(8,128)}) custom-call(f32[32]{0:T(128)} %slopes_ref.1, s32[8]{0:T(128)} %docs_ref.1, bf16[512,4096]{1,0:T(8,128)(2,1)} %q_hbm.1, bf16[512,4096]{1,0:T(8,128)(2,1)} %k_hbm.1, bf16[512,4096]{1,0:T(8,128)(2,1)} %v_hbm.1), custom_call_target="tpu_custom_call" | custom-call | tf_op jit(solution)/shard_map/pallas_call | solution.py:370
  40.6 7.1 %shard_map.65 = bf16[512,4096]{1,0:T(8,128)(2,1)} custom-call(bf16[512,4096]{1,0:T(8,128)(2,1)} %get-tuple-element.7.mixed_ref, f32[512,128]{1,0:T(8,128)} %get-tuple-element.8.inv_ref, f32[1,4096]{1,0:T(1,128)} %bitcast.1), custom_call_target="tpu_custom_call" | custom-call | tf_op jit(solution)/shard_map/pallas_call | solution.py:407

commit v3 on v2

--- a/solution.py
+++ b/solution.py
@@ -16,18 +16,20 @@
 
 
 def kernel(
-    planes, head_parts, heads, blocks, parts,
+    planes, head_parts, heads, blocks, step, few,
     slopes_ref, docs_ref, q_hbm, k_hbm, v_hbm,
     mixed_hbm, inv_ref,
-    q_ref, k_ref, v_ref, mixed_ref, out_ref, local_ref, own_ref, carry_ref,
-    s_send, s_recv, p_send, p_recv, x_recv, c_send, c_recv,
+    q_ref, k_ref, v_ref, mixed_ref, out_ref, local_ref, own_ref, carry_ref, chip_ref,
+    s_send, s_recv, c_send, c_recv, a_send, a_recv, p_send, p_recv, x_send, x_recv,
     lag_ref, same_ref, tail_ref, lead_ref, rem_ref, reach_ref, sq_ref, sq_send, sq_recv,
     q_sem, k_sem, v_sem, o_sem,
-    s_out, s_in, p_out, p_in, x_out, x_in, c_out, c_in, sq_out, sq_in,
+    s_out, s_in, c_out, c_in, a_out, a_in, p_out, p_in, x_out, x_in, sq_out, sq_in,
 ):
     half = heads // 2
-    step = half // parts
+    quarter = half // 2
+    parts = half // step
     chunks = 2 * parts
+    turns = quarter // few
     rows = blocks * BLOCK
     size = q_ref.shape[1] // heads
     seq = lax.axis_index("seq")
@@ -38,10 +40,17 @@
     partner = seq + 1 - 2 * core
     across = seq + 2 - 4 * side
     ahead = jnp.minimum(seq + 4, 4 * planes - 1)
-    first = (1 - core) * half
+    far = (1 - side) * quarter
+
+    def mine(u):
+        return core * half + lax.rem(u + far, half)
+
+    def theirs(u):
+        return (1 - core) * half + lax.rem(u + far, half)
 
     def head_of(o):
-        return lax.rem(o + first, heads)
+        group = jnp.where(o >= half, core, 1 - core)
+        return group * half + lax.rem(lax.rem(o, half) + far, half)
 
     def cols(h):
         return pl.ds(pl.multiple_of(h * size, size), size)
@@ -55,27 +64,28 @@
     def store(oc):
         return pltpu.make_async_copy(out_ref.at[:, wide(oc)], mixed_hbm.at[:, wide(oc)], o_sem.at[oc])
 
-    def piece(c):
-        return pl.ds(c * step, step)
-
-    def remote(src, dst, c, out_sem, in_sem, target):
+    def remote(src, dst, c, count, out_sem, in_sem, target):
+        piece = pl.ds(c * count, count)
         return pltpu.make_async_remote_copy(
-            src_ref=src.at[piece(c)], dst_ref=dst.at[piece(c)],
+            src_ref=src.at[piece], dst_ref=dst.at[piece],
             send_sem=out_sem.at[c], recv_sem=in_sem.at[c],
             device_id={"seq": target}, device_id_type=MESH,
         )
 
     def s_copy(c):
-        return remote(s_send, s_recv, c, s_out, s_in, partner)
+        return remote(s_send, s_recv, c, step, s_out, s_in, partner)
+
+    def c_copy(c):
+        return remote(c_send, c_recv, c, few, c_out, c_in, partner)
+
+    def a_copy(c):
+        return remote(a_send, a_recv, c, few, a_out, a_in, across)
 
     def p_copy(c):
-        return remote(p_send, p_recv, c, p_out, p_in, ahead)
-
-    def x_copy(c, src):
-        return remote(src, x_recv, c, x_out, x_in, across)
-
-    def c_copy(c):
-        return remote(c_send, c_recv, c, c_out, c_in, partner)
+        return remote(p_send, p_recv, c, few, p_out, p_in, ahead)
+
+    def x_copy(c):
+        return remote(x_send, x_recv, c, few, x_out, x_in, across)
 
     def each(count, body, start=0):
         def turn(i, _):
@@ -83,9 +93,9 @@
             return 0
         lax.fori_loop(start, count, turn, 0)
 
-    def grouped(c, body):
-        for i in range(step):
-            body(c * step + i)
+    def grouped(c, body, count=step):
+        for i in range(count):
+            body(c * count + i)
 
     barrier = pltpu.get_barrier_semaphore()
     pl.semaphore_signal(barrier, inc=1, device_id={"seq": partner}, device_id_type=MESH)
@@ -143,10 +153,12 @@
         tail_ref[b] = jnp.where(row_seg == segment(b0 + BLOCK - 1), F32(1), F32(0))
         lead_ref[b] = jnp.where(row_seg == segment(b0 - 1), F32(1), F32(0))
         within.append(joined(b0 - 1, b0 + BLOCK - 1))
+    board = chip - 2 * side * rows
     j_cores = joined(chip + rows - 1, chip + 2 * rows - 1)
-    j_first = joined(chip - 1, chip + rows - 1)
-    j_chain = joined(chip - 2 * rows - 1, chip + 2 * rows - 1)
-    j_skip = joined(chip - 2 * rows - 1, chip - 1)
+    j_enter = joined(chip - 1, chip + rows - 1)
+    j_chips = joined(board + 2 * rows - 1, board + 4 * rows - 1)
+    j_board = joined(board - 1, board + 4 * rows - 1)
+    j_front = joined(board - 1, board + 2 * rows - 1)
 
     def rate(h):
         return slopes_ref[h] * F32(-LOG2E)
@@ -179,10 +191,10 @@
         load(v_hbm, v_ref, v_sem, oc).wait()
 
     def give(i):
-        s_send[i] = end_state(first + i).astype(BF16)
+        s_send[i] = end_state(theirs(i)).astype(BF16)
 
     def keep(i):
-        own_ref[i] = end_state(core * half + i)
+        own_ref[i] = end_state(mine(i))
 
     def first_chunk(c):
         wait_kv(c)
@@ -229,55 +241,79 @@
         grouped(oc, lambda o: intra(head_of(o)))
 
     is_second = core == 1
-
-    def chip_states(i):
-        mine, other = own_ref[i], s_recv[i].astype(F32)
-        return jnp.where(is_second, other, mine), jnp.where(is_second, mine, other)
-
-    def chain(i):
-        h = core * half + i
-        early, late = chip_states(i)
-        chip_state = fade(h, F32(rows), j_cores) * early + late
-        p_send[i] = (fade(h, F32(4 * rows), j_chain) * p_recv[i].astype(F32) + chip_state).astype(BF16)
+    is_after = side == 1
+
+    def core_states(u):
+        here, there = own_ref[u], s_recv[u].astype(F32)
+        return jnp.where(is_second, there, here), jnp.where(is_second, here, there)
+
+    def chip_state(u):
+        early, late = core_states(u)
+        return fade(mine(u), F32(rows), j_cores) * early + late
+
+    def give_chip(w):
+        a_send[w] = chip_state(w).astype(BF16)
+
+    def keep_chip(w):
+        chip_ref[w] = chip_state(quarter + w)
+
+    def give_chunk(c):
+        s_copy(c).wait_recv()
+        grouped(c, give_chip)
+        for i in range(step // few):
+            a_copy(c * (step // few) + i).start()
+
+    each(parts // 2, give_chunk)
+
+    def keep_chunk(c):
+        s_copy(parts // 2 + c).wait_recv()
+        grouped(c, keep_chip)
+
+    each(parts // 2, keep_chunk)
+
+    def settle(u, enters):
+        early, _ = core_states(u)
+        second = fade(mine(u), F32(rows), j_enter) * enters + early
+        carry_ref[u] = jnp.where(is_second, second, enters)
+        c_send[u] = jnp.where(is_second, enters, second).astype(BF16)
+
+    def chain(w):
+        h = mine(quarter + w)
+        here, there = chip_ref[w], a_recv[w].astype(F32)
+        early, late = jnp.where(is_after, there, here), jnp.where(is_after, here, there)
+        before = p_recv[w].astype(F32)
+        total = fade(h, F32(2 * rows), j_chips) * early + late
+        p_send[w] = (fade(h, F32(4 * rows), j_board) * before + total).astype(BF16)
+        second = fade(h, F32(2 * rows), j_front) * before + early
+        x_send[w] = jnp.where(is_after, before, second).astype(BF16)
+        settle(quarter + w, jnp.where(is_after, second, before))
 
     def chain_chunk(c):
-        s_copy(c).wait_recv()
+        a_copy(c).wait_recv()
 
         @pl.when(plane > 0)
         def _():
             p_copy(c).wait_recv()
 
-        @pl.when(side == 1)
-        def _():
-            x_copy(c, p_recv).start()
-
-        grouped(c, chain)
+        grouped(c, chain, few)
 
         @pl.when(plane < planes - 1)
         def _():
             p_copy(c).start()
 
-        @pl.when(side == 0)
-        def _():
-            x_copy(c, p_send).start()
-
-    head_start = jnp.minimum(plane, parts)
-    each(head_start, intra_chunk)
-
-    def chain_and_intra(c):
-        chain_chunk(c)
-        intra_chunk(head_start + c)
-
-    each(parts, chain_and_intra)
-    each(chunks, intra_chunk, head_start + parts)
-
-    def settle(i):
-        h = core * half + i
-        early, _ = chip_states(i)
-        enters = fade(h, F32(2 * rows), j_skip) * p_recv[i].astype(F32) + x_recv[i].astype(F32)
-        second = fade(h, F32(rows), j_first) * enters + early
-        carry_ref[i] = jnp.where(is_second, second, enters)
-        c_send[i] = jnp.where(is_second, enters, second).astype(BF16)
+        x_copy(c).start()
+        c_copy(turns + c).start()
+
+    def across_chunk(c):
+        x_copy(c).wait_recv()
+        grouped(c, lambda w: settle(w, x_recv[w].astype(F32)), few)
+        c_copy(c).start()
+
+    ready = jnp.minimum(2 + 2 * plane, chunks)
+    each(ready, intra_chunk)
+    each(turns, chain_chunk)
+    each(chunks, intra_chunk, ready)
+    each(turns, across_chunk)
 
     def finish_all(work):
         fades = [jnp.exp2(reach_ref[...] * rate(h)) for h, _ in work]
@@ -296,21 +332,21 @@
                     states[i] = fade(h, F32(BLOCK), within[b]) * states[i] + local_ref[b, h]
             sq_ref[here, :] = squares
 
-    def settle_chunk(c):
-        x_copy(c, p_recv).wait_recv()
-        grouped(c, settle)
-        c_copy(c).start()
-        finish_all([(core * half + c * step + i, carry_ref[c * step + i]) for i in range(step)])
+    def own_part(c):
+        finish_all([(mine(c * step + i), carry_ref[c * step + i]) for i in range(step)])
         store(parts + c).start()
 
-    each(parts, settle_chunk)
-
-    def last_chunk(c):
-        c_copy(c).wait_recv()
-        finish_all([(first + c * step + i, c_recv[c * step + i].astype(F32)) for i in range(step)])
+    each(parts, own_part)
+
+    def other_part(c):
+        for i in range(step // few):
+            c_copy(c * (step // few) + i).wait_recv()
+        finish_all(
+            [(theirs(c * step + i), c_recv[c * step + i].astype(F32)) for i in range(step)]
+        )
         store(c).start()
 
-    each(parts, last_chunk)
+    each(parts, other_part)
 
     ones = jnp.ones((8, size), F32)
     summed = lax.dot_general(
@@ -328,16 +364,18 @@
     for i in range(1, head_parts):
         sq_copy(i).start()
 
+    each(parts, lambda c: s_copy(c).wait_send())
+    each(2 * turns, lambda c: c_copy(c).wait_send())
+
     def drain(c):
-        s_copy(c).wait_send()
-        x_copy(c, p_send).wait_send()
-        c_copy(c).wait_send()
+        a_copy(c).wait_send()
+        x_copy(c).wait_send()
 
         @pl.when(plane < planes - 1)
         def _():
             p_copy(c).wait_send()
 
-    each(parts, drain)
+    each(turns, drain)
     for i in range(1, head_parts):
         sq_copy(i).wait_recv()
         summed = summed + sq_recv[i]
@@ -362,13 +400,17 @@
     size = feat // heads
     blocks = rows // BLOCK
     half = heads // 2
-    parts = min(4, half)
+    quarter = half // 2
+    step = min(4, quarter)
+    few = max(1, quarter // 4)
+    parts = half // step
+    turns = quarter // few
     hbm = pl.BlockSpec(memory_space=pl.ANY)
     smem = pl.BlockSpec(memory_space=pltpu.SMEM)
-    states = lambda dtype: pltpu.VMEM((half, size, size), dtype)
+    states = lambda count, dtype: pltpu.VMEM((count, size, size), dtype)
     dma = lambda n: pltpu.SemaphoreType.DMA((n,))
     mixed, inverse = pl.pallas_call(
-        functools.partial(kernel, planes, head_parts, heads, blocks, parts),
+        functools.partial(kernel, planes, head_parts, heads, blocks, step, few),
         out_shape=(
             jax.ShapeDtypeStruct((rows, feat), BF16),
             jax.ShapeDtypeStruct((rows, size), F32),
@@ -382,9 +424,11 @@
             pltpu.VMEM((rows, feat), F32),
             pltpu.VMEM((rows, feat), BF16),
             pltpu.VMEM((max(blocks - 1, 1), heads, size, size), F32),
-            states(F32),
-            states(F32),
-            *[states(BF16)] * 7,
+            states(half, F32),
+            states(half, F32),
+            states(quarter, F32),
+            *[states(half, BF16)] * 4,
+            *[states(quarter, BF16)] * 6,
             pltpu.VMEM((BLOCK // 2, BLOCK), F32),
             pltpu.VMEM((blocks, BLOCK, BLOCK), F32),
             pltpu.VMEM((blocks, BLOCK, size), F32),
@@ -395,7 +439,9 @@
             pltpu.VMEM((8, rows), F32),
             pltpu.VMEM((head_parts, 8, rows), F32),
             *[dma(2 * parts)] * 4,
-            *[dma(parts)] * 8,
+            *[dma(parts)] * 2,
+            *[dma(2 * turns)] * 2,
+            *[dma(turns)] * 6,
             dma(head_parts),
             dma(head_parts),
         ],

time: 48 us -> 43.1 us (0.90)
  Pallas kernels: 47.7 us -> 42.8 us
    pallas_call x1, Pallas kernels: 40.6 us -> 35.7 us  [shards(): pl.pallas_call(functools.partial(kernel, planes, head_parts, heads, block...]
where the time goes in v3:
time: 43.1 us; the launch traced here: 42.8 us
  Pallas kernels  42.8 us (99%)
    pallas_call x1, Pallas kernels, shards(): pl.pallas_call(functools.partial(kernel, planes, head_parts, heads, block...  35.7 us
    pallas_call x1, Pallas kernels, shards(): pl.pallas_call(scale_kernel, out_shape=jax.ShapeDtypeStruct((rows, feat),...  7.1 us

profile of v3, /device:TPU:24, one launch (start us, length us, event | category | flops | bytes accessed | tf_op | source)
XLA Modules:
  0.0 42.8 jit_solution(17762756880321114787)
XLA Ops:
  0.0 35.7 %shard_map.64 = (bf16[512,4096]{1,0:T(8,128)(2,1)}, f32[512,128]{1,0:T(8,128)}) custom-call(f32[32]{0:T(128)} %slopes_ref.1, s32[8]{0:T(128)} %docs_ref.1, bf16[512,4096]{1,0:T(8,128)(2,1)} %q_hbm.1, bf16[512,4096]{1,0:T(8,128)(2,1)} %k_hbm.1, bf16[512,4096]{1,0:T(8,128)(2,1)} %v_hbm.1), custom_call_target="tpu_custom_call" | custom-call | tf_op jit(solution)/shard_map/pallas_call | solution.py:412
  35.7 7.1 %shard_map.65 = bf16[512,4096]{1,0:T(8,128)(2,1)} custom-call(bf16[512,4096]{1,0:T(8,128)(2,1)} %get-tuple-element.7.mixed_ref, f32[512,128]{1,0:T(8,128)} %get-tuple-element.8.inv_ref, f32[1,4096]{1,0:T(1,128)} %bitcast.1), custom_call_target="tpu_custom_call" | custom-call | tf_op jit(solution)/shard_map/pallas_call | solution.py:453

commit v4 on v3

--- a/solution.py
+++ b/solution.py
@@ -18,11 +18,11 @@
 def kernel(
     planes, head_parts, heads, blocks, step, few,
     slopes_ref, docs_ref, q_hbm, k_hbm, v_hbm,
-    mixed_hbm, inv_ref,
-    q_ref, k_ref, v_ref, mixed_ref, out_ref, local_ref, own_ref, carry_ref, chip_ref,
+    out_ref, inv_ref,
+    q_ref, k_ref, v_ref, mixed_ref, local_ref, own_ref, carry_ref, chip_ref,
     s_send, s_recv, c_send, c_recv, a_send, a_recv, p_send, p_recv, x_send, x_recv,
     lag_ref, same_ref, tail_ref, lead_ref, rem_ref, reach_ref, sq_ref, sq_send, sq_recv,
-    q_sem, k_sem, v_sem, o_sem,
+    q_sem, k_sem, v_sem,
     s_out, s_in, c_out, c_in, a_out, a_in, p_out, p_in, x_out, x_in, sq_out, sq_in,
 ):
     half = heads // 2
@@ -60,9 +60,6 @@
 
     def load(hbm, ref, sem, oc):
         return pltpu.make_async_copy(hbm.at[:, wide(oc)], ref.at[:, wide(oc)], sem.at[oc])
-
-    def store(oc):
-        return pltpu.make_async_copy(out_ref.at[:, wide(oc)], mixed_hbm.at[:, wide(oc)], o_sem.at[oc])
 
     def remote(src, dst, c, count, out_sem, in_sem, target):
         piece = pl.ds(c * count, count)
@@ -334,7 +331,6 @@
 
     def own_part(c):
         finish_all([(mine(c * step + i), carry_ref[c * step + i]) for i in range(step)])
-        store(parts + c).start()
 
     each(parts, own_part)
 
@@ -344,7 +340,6 @@
         finish_all(
             [(theirs(c * step + i), c_recv[c * step + i].astype(F32)) for i in range(step)]
         )
-        store(c).start()
 
     each(parts, other_part)
 
@@ -383,15 +378,25 @@
     inv_ref[...] = jnp.broadcast_to(jnp.transpose(inverse)[:, 0:1], inv_ref.shape)
     for i in range(1, head_parts):
         sq_copy(i).wait_send()
-    each(chunks, lambda oc: store(oc).wait())
-
-
-def scale_kernel(mixed_ref, inv_ref, gain_ref, out_ref):
-    size = inv_ref.shape[1]
-    inverse = inv_ref[...]
-    for c in range(0, out_ref.shape[1], size):
-        piece = mixed_ref[:, c:c + size].astype(F32)
-        out_ref[:, c:c + size] = (piece * inverse * gain_ref[:, c:c + size]).astype(BF16)
+
+
+def scale_kernel(mixed_ref, inv_ref, gain_ref, final_hbm, final_ref, sem):
+    rows, size = inv_ref.shape
+    strip = rows // sem.shape[0]
+
+    def move(i):
+        here = pl.ds(i * strip, strip)
+        return pltpu.make_async_copy(final_ref.at[here], final_hbm.at[here], sem.at[i])
+
+    for i in range(sem.shape[0]):
+        here = pl.ds(i * strip, strip)
+        inverse = inv_ref[here, :]
+        for c in range(0, final_ref.shape[1], size):
+            piece = mixed_ref[here, c:c + size].astype(F32)
+            final_ref[here, c:c + size] = (piece * inverse * gain_ref[:, c:c + size]).astype(BF16)
+        move(i).start()
+    for i in range(sem.shape[0]):
+        move(i).wait()
 
 
 def shards(planes, head_parts, queries, key_rows, values, slopes, doc_lengths, norm_gain):
@@ -402,10 +407,10 @@
     half = heads // 2
     quarter = half // 2
     step = min(4, quarter)
-    few = max(1, quarter // 4)
+    few = max(1, quarter // 8)
     parts = half // step
     turns = quarter // few
-    hbm = pl.BlockSpec(memory_space=pl.ANY)
+    hbm = pl.BlockSpec(memory_space=pltpu.HBM)
     smem = pl.BlockSpec(memory_space=pltpu.SMEM)
     states = lambda count, dtype: pltpu.VMEM((count, size, size), dtype)
     dma = lambda n: pltpu.SemaphoreType.DMA((n,))
@@ -416,13 +421,12 @@
             jax.ShapeDtypeStruct((rows, size), F32),
         ),
         in_specs=[smem, smem, hbm, hbm, hbm],
-        out_specs=(hbm, pl.BlockSpec(memory_space=pltpu.VMEM)),
+        out_specs=(pl.BlockSpec(memory_space=pltpu.VMEM), pl.BlockSpec(memory_space=pltpu.VMEM)),
         scratch_shapes=[
             pltpu.VMEM((rows, feat), BF16),
             pltpu.VMEM((rows, feat), BF16),
             pltpu.VMEM((rows, feat), BF16),
             pltpu.VMEM((rows, feat), F32),
-            pltpu.VMEM((rows, feat), BF16),
             pltpu.VMEM((max(blocks - 1, 1), heads, size, size), F32),
             states(half, F32),
             states(half, F32),
@@ -438,7 +442,7 @@
             pltpu.VMEM((rows, size), F32),
             pltpu.VMEM((8, rows), F32),
             pltpu.VMEM((head_parts, 8, rows), F32),
-            *[dma(2 * parts)] * 4,
+            *[dma(2 * parts)] * 3,
             *[dma(parts)] * 2,
             *[dma(2 * turns)] * 2,
             *[dma(turns)] * 6,
@@ -446,20 +450,17 @@
             dma(head_parts),
         ],
         compiler_params=pltpu.CompilerParams(
-            collective_id=0, has_side_effects=True, vmem_limit_bytes=56 * 1024 * 1024
+            collective_id=0, has_side_effects=True, vmem_limit_bytes=47 * 1024 * 1024
         ),
     )(slopes, doc_lengths, queries, key_rows, values)
-    width = feat // 8
+    vmem = pl.BlockSpec(memory_space=pltpu.VMEM)
     return pl.pallas_call(
         scale_kernel,
         out_shape=jax.ShapeDtypeStruct((rows, feat), BF16),
-        grid=(feat // width,),
-        in_specs=[
-            pl.BlockSpec((rows, width), lambda i: (0, i)),
-            pl.BlockSpec((rows, size), lambda i: (0, 0)),
-            pl.BlockSpec((1, width), lambda i: (0, i)),
-        ],
-        out_specs=pl.BlockSpec((rows, width), lambda i: (0, i)),
+        in_specs=[vmem, vmem, vmem],
+        out_specs=pl.BlockSpec(memory_space=pltpu.HBM),
+        scratch_shapes=[pltpu.VMEM((rows, feat), BF16), pltpu.SemaphoreType.DMA((8,))],
+        compiler_params=pltpu.CompilerParams(vmem_limit_bytes=9 * 1024 * 1024),
     )(mixed, inverse, norm_gain.reshape(1, feat))
 
 

time: 43.1 us -> 37.3 us (0.87)
  Pallas kernels: 42.8 us -> 35.8 us
  local copies, waits for them, and re-layouts: 0 us -> 1.31 us
    pallas_call x1, Pallas kernels: 7.1 us -> 2.21 us  [shards(): pl.pallas_call(scale_kernel, out_shape=jax.ShapeDtypeStruct((rows, feat),...]
    pallas_call x1, Pallas kernels: 35.7 us -> 33.5 us  [shards(): pl.pallas_call(functools.partial(kernel, planes, head_parts, heads, block...]
    unnamed x0 -> x6, local copies, waits for them, and re-layouts: none -> 1.31 us
where the time goes in v4:
time: 37.3 us; the launch traced here: 37.1 us
  Pallas kernels  35.8 us (96%)
  local copies, waits for them, and re-layouts  1.31 us (4%)
    pallas_call x1, Pallas kernels, shards(): pl.pallas_call(functools.partial(kernel, planes, head_parts, heads, block...  33.5 us
    pallas_call x1, Pallas kernels, shards(): pl.pallas_call(scale_kernel, out_shape=jax.ShapeDtypeStruct((rows, feat),...  2.21 us
    unnamed x6, local copies, waits for them, and re-layouts  1.31 us

profile of v4, /device:TPU:24, one launch (start us, length us, event | category | flops | bytes accessed | tf_op | source)
XLA Modules:
  0.0 37.1 jit_solution(5991985410231173743)
XLA Ops:
  0.0 0.0 copy-start.1
  0.0 0.7 %copy-done.1 = f32[32]{0:T(128)S(1)} copy-done((f32[32]{0:T(128)S(1)}, f32[32]{0:T(128)}, u32[]{:S(2)}) %copy-start.1) | copy-done | bytes 152
  0.7 0.0 copy-start.2
  0.7 0.7 %copy-done.2 = s32[8]{0:T(128)S(1)} copy-done((s32[8]{0:T(128)S(1)}, s32[8]{0:T(128)}, u32[]{:S(2)}) %copy-start.2) | copy-done | bytes 56
  1.3 0.0 copy-start
  1.3 33.5 %shard_map.64 = (bf16[512,4096]{1,0:T(8,128)(2,1)S(1)}, f32[512,128]{1,0:T(8,128)S(1)}) custom-call(f32[32]{0:T(128)S(1)} %copy-done.1, s32[8]{0:T(128)S(1)} %copy-done.2, bf16[512,4096]{1,0:T(8,128)(2,1)} %q_hbm.1, bf16[512,4096]{1,0:T(8,128)(2,1)} %k_hbm.1, bf16[512,4096]{1,0:T(8,128)(2,1)} %v_hbm.1), custom_call_target="tpu_custom_call" | custom-call | tf_op jit(solution)/shard_map/pallas_call | solution.py:417
  34.9 0.0 copy-done
  34.9 2.2 %shard_map.65 = bf16[512,4096]{1,0:T(8,128)(2,1)} custom-call(bf16[512,4096]{1,0:T(8,128)(2,1)S(1)} %get-tuple-element.7.mixed_ref, f32[512,128]{1,0:T(8,128)S(1)} %get-tuple-element.8.inv_ref, f32[1,4096]{1,0:T(1,128)S(1)} %bitcast.1), custom_call_target="tpu_custom_call" | custom-call | tf_op jit(solution)/shard_map/pallas_call | solution.py:457
Async XLA Ops:
  0.0 0.7 %copy-start.1 = (f32[32]{0:T(128)S(1)}, f32[32]{0:T(128)}, u32[]{:S(2)}) copy-start(f32[32]{0:T(128)} %slopes_ref.1) | copy-start | bytes 388
  0.7 0.7 %copy-start.2 = (s32[8]{0:T(128)S(1)}, s32[8]{0:T(128)}, u32[]{:S(2)}) copy-start(s32[8]{0:T(128)} %docs_ref.1) | copy-start | bytes 100
  1.3 33.6 %copy-start = (f32[4096]{0:T(1024)S(1)}, f32[4096]{0:T(1024)}, u32[]{:S(2)}) copy-start(f32[4096]{0:T(1024)} %param.11) | copy-start | bytes 49156
